TPU v7x, 32 devices: a whole 2x2x4 slice. The times are simulated.
32 devices in a mesh: band: 4 (over y, core), grid: 8 (over z, x).
Axes of the slice: x: 2, y: 2, z: 4, core: 2. Of those that a mesh axis runs over, the one named last changes fastest.
Arguments:
- orbitals: float32 [64, 16, 4096], P('band', 'grid'), may hold values from -6 to 6
- potential: float32 [16, 4096], P('grid'), may hold values from 0 to 2
Outputs:
- rotated: bfloat16 [64, 16, 4096], P('band', 'grid')
All inputs are finite; a program needn't handle non-finite values. Where the computation divides by a largest or mean magnitude, that divisor is 1e-20 or more.
Results may differ from a plain program's by a relative error of at most 0.001.
The roundings to bfloat16 on the way count: a program that leaves them out, or rounds other values in their place, can miss the bound.
Values may be sent and summed in bfloat16 or wider, within the bound.
A program may use at most 64 MiB of HBM per device.

v0:
```python
import jax
import jax.numpy as jnp
from jax import lax
from jax.sharding import PartitionSpec as P

NX = 64
DEGREE = 2
NS_ITERS = 2


def with_halo(block, sides, width):
    for axis, dim in sides:
        count = lax.axis_size(axis)
        forward = [(i, i + 1) for i in range(count - 1)]
        forward.append((count - 1, 0))
        backward = [(target, source) for source, target in forward]
        low = lax.ppermute(
            lax.slice_in_dim(block, block.shape[dim] - width, None, axis=dim), axis, forward
        )
        high = lax.ppermute(lax.slice_in_dim(block, 0, width, axis=dim), axis, backward)
        block = jnp.concatenate([low, block, high], axis=dim)
    return block


def apply_inner(extended, potential):
    inner = extended[:, 1:-1]
    count = inner.shape[0]
    planes = inner.shape[1]
    square = inner.reshape(count, planes, NX, NX)
    sideways = jnp.roll(square, 1, 2) + jnp.roll(square, -1, 2)
    sideways = sideways + jnp.roll(square, 1, 3) + jnp.roll(square, -1, 3)
    beside = extended[:, 2:] + extended[:, :-2] + sideways.reshape(inner.shape)
    return 0.5 * (6.0 * inner - beside) + potential[None] * inner


def local(orbitals, potential):
    previous = orbitals
    current = orbitals
    for degree_step in range(DEGREE):
        extended = with_halo(current, (("grid", 1),), 1)
        applied = apply_inner(extended, potential)
        if degree_step == 0:
            following = (applied - 5.0 * current) / 3.0
        else:
            following = 2.0 * (applied - 5.0 * current) / 3.0 - previous
        previous = current
        current = following
    count, zplanes, width = orbitals.shape
    filtered = current.astype(jnp.bfloat16).reshape(count, zplanes * width)
    pieces = lax.all_to_all(filtered, "band", split_axis=1, concat_axis=0, tiled=True)
    total_cells = pieces.shape[1] * lax.axis_size("band") * lax.axis_size("grid")
    partial_value = (
        lax.dot_general(
            pieces, pieces, (((1,), (1,)), ((), ())), preferred_element_type=jnp.float32
        )
        / total_cells
    )
    gram = lax.psum(partial_value, ("band", "grid"))
    scale = jnp.max(jnp.sum(jnp.abs(gram), axis=1))
    identity_mat = jnp.eye(gram.shape[0], dtype=jnp.float32)
    upper = gram / scale
    lower = identity_mat
    for sweep in range(NS_ITERS):
        factor = 1.5 * identity_mat - 0.5 * jnp.dot(lower, upper, precision=lax.Precision.HIGHEST)
        upper = jnp.dot(upper, factor, precision=lax.Precision.HIGHEST)
        lower = jnp.dot(factor, lower, precision=lax.Precision.HIGHEST)
    root = (lower / jnp.sqrt(scale)).astype(jnp.bfloat16)
    turned = lax.dot_general(
        root, pieces, (((0,), (0,)), ((), ())), preferred_element_type=jnp.float32
    )
    turned = turned.astype(jnp.bfloat16)
    returned = lax.all_to_all(turned, "band", split_axis=0, concat_axis=1, tiled=True)
    return returned.reshape(count, zplanes, width)


def solution(mesh):
    placed = (P("band", "grid", None), P("grid", None))
    return jax.shard_map(
        local, mesh=mesh, in_specs=placed, out_specs=P("band", "grid", None), check_vma=False
    )
```

profile of v0, /device:TPU:0, one launch (start us, length us, event | category | flops | bytes accessed | tf_op | source)
XLA Modules:
  0.0 102.4 jit_solution(3121627851999156750)
XLA Ops:
  0.0 1.9 %fusion.24 = (f32[16,1,4096]{2,1,0:T(1,128)S(1)}, f32[16,1,4096]{2,1,0:T(1,128)S(1)}) fusion(f32[16,2,4096]{2,1,0:T(2,128)} %param.2), kind=kLoop, calls=%fused_computation.42 | loop fusion | bytes 1048576 | tf_op jit(solution)/shard_map/slice | solution.py:20
  1.9 6.1 %collective-permute-start = (f32[16,1,4096]{2,1,0:T(1,128)S(1)}, f32[16,1,4096]{2,1,0:T(1,128)S(1)}, u32[]{:S(2)}, u32[]{:S(2)}) collective-permute-start(f32[16,1,4096]{2,1,0:T(1,128)S(1)} %get-tuple-element.25), channel_id=1, source_target_pairs={{1,0},{2,1},{3,2},{4,3},{5,4},{6,5},{7,6},{0,7},{9,8},{10,9},{11,1... | collective-permute-start | bytes 786440 | tf_op jit(solution)/shard_map/ppermute | solution.py:20
  7.9 0.6 reshape.35
  8.6 0.4 fusion.19
  9.5 0.5 copy-done.1
  10.1 0.9 fusion.4
  11.0 0.5 add.58
  11.5 2.0 %collective-permute-done = f32[16,1,4096]{2,1,0:T(1,128)S(1)} collective-permute-done((f32[16,1,4096]{2,1,0:T(1,128)S(1)}, f32[16,1,4096]{2,1,0:T(1,128)S(1)}, u32[]{:S(2)}, u32[]{:S(2)}) %collective-permute-start) | collective-permute-done | bytes 262176 | tf_op jit(solution)/shard_map/ppermute | solution.py:20
  13.5 5.0 %collective-permute-done.1 = f32[16,1,4096]{2,1,0:T(1,128)} collective-permute-done((f32[16,1,4096]{2,1,0:T(1,128)S(1)}, f32[16,1,4096]{2,1,0:T(1,128)}, u32[]{:S(2)}, u32[]{:S(2)}) %collective-permute-start.1) | collective-permute-done | bytes 262176 | tf_op jit(solution)/shard_map/ppermute | solution.py:17
  18.5 2.4 %broadcast_multiply_fusion = (f32[16,2,4096]{2,1,0:T(2,128)S(1)}, f32[16,2,4096]{2,1,0:T(2,128)S(1)}) fusion(f32[16,2,4096]{2,1,0:T(2,128)S(1)} %copy-done, f32[2,4096]{1,0:T(2,128)S(1)} %copy-done.1, f32[16,2,4096]{2,1,0:T(2,128)S(1)} %add.58, f32[16,1,4096]{2,1,0:T(1,128)} %collective-permute-done.1, f32[16,1,4096]{2,1,0:T(1,128)S(1)} %collective-permute-done), kind=kLoop, calls=%fused_computation.26 | loop fusion | flops 1572864 | bytes 2654208 | tf_op jit(solution)/shard_map/div | solution.py:43
  21.0 0.6 reshape.36
  22.5 1.3 %fusion.23 = (f32[16,1,4096]{2,1,0:T(1,128)}, f32[16,1,4096]{2,1,0:T(1,128)}) fusion(f32[16,2,4096]{2,1,0:T(2,128)S(1)} %get-tuple-element.5), kind=kLoop, calls=%fused_computation.41 | loop fusion | bytes 1048576 | tf_op jit(solution)/shard_map/slice | solution.py:20
  23.9 3.5 %collective-permute-start.2 = (f32[16,1,4096]{2,1,0:T(1,128)}, f32[16,1,4096]{2,1,0:T(1,128)S(1)}, u32[]{:S(2)}, u32[]{:S(2)}) collective-permute-start(f32[16,1,4096]{2,1,0:T(1,128)} %get-tuple-element.23), channel_id=1, source_target_pairs={{1,0},{2,1},{3,2},{4,3},{5,4},{6,5},{7,6},{0,7},{9,8},{10,9},{11,1... | collective-permute-start | bytes 786440 | tf_op jit(solution)/shard_map/ppermute | solution.py:20
  27.4 0.9 fusion.6
  28.2 0.5 add.65
  28.8 8.5 %collective-permute-done.2 = f32[16,1,4096]{2,1,0:T(1,128)S(1)} collective-permute-done((f32[16,1,4096]{2,1,0:T(1,128)}, f32[16,1,4096]{2,1,0:T(1,128)S(1)}, u32[]{:S(2)}, u32[]{:S(2)}) %collective-permute-start.2) | collective-permute-done | bytes 262176 | tf_op jit(solution)/shard_map/ppermute | solution.py:20
  37.5 2.6 %subtract_convert_fusion = bf16[16,2,4096]{2,1,0:T(2,128)(2,1)S(1)} fusion(f32[16,2,4096]{2,1,0:T(2,128)S(1)} %copy-done, f32[16,2,4096]{2,1,0:T(2,128)S(1)} %get-tuple-element.6, f32[16,2,4096]{2,1,0:T(2,128)S(1)} %add.65, f32[16,2,4096]{2,1,0:T(2,128)S(1)} %get-tuple-element.5, f32[16,1,4096]{2,1,0:T(1,128)} %collective-permute-done.3, ...), kind=kLoop, calls=%fused_computation.24 | loop fusion | flops 1835008 | bytes 2916352 | tf_op jit(solution)/shard_map/convert_element_type | solution.py:49
  40.3 8.6 %all_to_all.35 = bf16[16,4,2048]{2,0,1:T(8,128)(2,1)S(1)} all-to-all(bf16[16,4,2048]{2,0,1:T(8,128)(2,1)S(1)} %copy.7), channel_id=1, replica_groups=mesh['band'=4,'grid'=8] {'band'}, dimensions={1} | all-to-all | bytes 524288 | tf_op jit(solution)/shard_map/all_to_all | solution.py:50
  49.1 39.0 %psum.7 = f32[64,64]{1,0:T(8,128)S(1)} all-reduce(f32[64,64]{1,0:T(8,128)S(1)} %convolution_multiply_fusion.2), channel_id=1, replica_groups=mesh['band'=4,'grid'=8] {'band','grid'}, use_global_device_ids=true, to_apply=%region_0.1 | all-reduce | flops 4096 | bytes 32768 | tf_op jit(solution)/shard_map/psum | solution.py:58
  88.2 0.6 reduce_max.9
  88.8 0.8 fusion.1
  89.6 0.8 fusion.14
  91.9 9.4 %all_to_all.36 = bf16[4,16,2048]{2,1,0:T(8,128)(2,1)S(1)} all-to-all(bf16[4,16,2048]{2,1,0:T(8,128)(2,1)S(1)} %bitcast.21), channel_id=1, replica_groups=mesh['band'=4,'grid'=8] {'band'}, dimensions={0} | all-to-all | bytes 524288 | tf_op jit(solution)/shard_map/all_to_all | solution.py:72
  101.5 0.9 reshape.37
  (23 shorter events, 3.3 us)
Async XLA Ops:
  0.0 7.9 %copy-start = (f32[16,2,4096]{2,1,0:T(2,128)S(1)}, f32[16,2,4096]{2,1,0:T(2,128)}, u32[]{:S(2)}) copy-start(f32[16,2,4096]{2,1,0:T(2,128)} %param.2) | copy-start | bytes 1572868
  1.9 11.6 %collective-permute-start = (f32[16,1,4096]{2,1,0:T(1,128)S(1)}, f32[16,1,4096]{2,1,0:T(1,128)S(1)}, u32[]{:S(2)}, u32[]{:S(2)}) collective-permute-start(f32[16,1,4096]{2,1,0:T(1,128)S(1)} %get-tuple-element.25), channel_id=1, source_target_pairs={{1,0},{2,1},{3,2},{4,3},{5,4},{6,5},{7,6},{0,7},{9,8},{10,9},{11,1... | collective-permute-start | bytes 786440 | tf_op jit(solution)/shard_map/ppermute | solution.py:20
  7.9 10.6 %collective-permute-start.1 = (f32[16,1,4096]{2,1,0:T(1,128)S(1)}, f32[16,1,4096]{2,1,0:T(1,128)}, u32[]{:S(2)}, u32[]{:S(2)}) collective-permute-start(f32[16,1,4096]{2,1,0:T(1,128)S(1)} %get-tuple-element.26), channel_id=1, source_target_pairs={{0,1},{1,2},{2,3},{3,4},{4,5},{5,6},{6,7},{7,0},{8,9},{9,10},{10,1... | collective-permute-start | bytes 786440 | tf_op jit(solution)/shard_map/ppermute | solution.py:17
  9.3 0.8 copy-start.1
  23.9 13.4 %collective-permute-start.2 = (f32[16,1,4096]{2,1,0:T(1,128)}, f32[16,1,4096]{2,1,0:T(1,128)S(1)}, u32[]{:S(2)}, u32[]{:S(2)}) collective-permute-start(f32[16,1,4096]{2,1,0:T(1,128)} %get-tuple-element.23), channel_id=1, source_target_pairs={{1,0},{2,1},{3,2},{4,3},{5,4},{6,5},{7,6},{0,7},{9,8},{10,9},{11,1... | collective-permute-start | bytes 786440 | tf_op jit(solution)/shard_map/ppermute | solution.py:20
  27.3 10.2 %collective-permute-start.3 = (f32[16,1,4096]{2,1,0:T(1,128)}, f32[16,1,4096]{2,1,0:T(1,128)}, u32[]{:S(2)}, u32[]{:S(2)}) collective-permute-start(f32[16,1,4096]{2,1,0:T(1,128)} %get-tuple-element.24), channel_id=1, source_target_pairs={{0,1},{1,2},{2,3},{3,4},{4,5},{5,6},{6,7},{7,0},{8,9},{9,10},{10,1... | collective-permute-start | bytes 786440 | tf_op jit(solution)/shard_map/ppermute | solution.py:17
where the time goes:
time: 103 us; the launch traced here: 102 us
  blocking collectives  56.9 us (55%)
  waiting for transfers between devices  15.7 us (15%)
  starting transfers between devices  9.52 us (9%)
  local copies, waits for them, and re-layouts  9.32 us (9%)
  other arithmetic  7.48 us (7%)
  matrix products  2.54 us (2%)
    psum x1, blocking collectives, local(): gram = lax.psum(partial_value, ('band', 'grid'))  39 us
    ppermute x2, waiting for transfers between devices, with_halo(): lax.ppermute(lax.slice_in_dim(block, 0, width, axis=dim), axis, backward)  10.5 us
    ppermute x2, starting transfers between devices, with_halo(): lax.ppermute(lax.slice_in_dim(block, 0, width, axis=dim), axis, backward)  9.51 us
    all_to_all x1, blocking collectives, local(): lax.all_to_all(turned, 'band', split_axis=0, concat_axis=1, tiled=True)  9.36 us
    all_to_all x1, blocking collectives, local(): lax.all_to_all(filtered, 'band', split_axis=1, concat_axis=0, tiled=True)  8.59 us
    ppermute x2, waiting for transfers between devices, with_halo(): lax.ppermute(lax.slice_in_dim(block, block.shape[dim] - width, None, axis...  5.27 us
    slice x2, local copies, waits for them, and re-layouts, with_halo(): lax.slice_in_dim(block, 0, width, axis=dim)  3.21 us
    convert_element_type x1, other arithmetic, local(): filtered = current.astype(jnp.bfloat16).reshape(count, zplanes * width)  2.58 us
  transfers between devices with their start and end apart: 4, of which 4 were waited for; matrix products, arithmetic and copies ran while one was open for 4% of the time, Pallas kernels for 0%

commit v1 on v0

--- a/solution.py
+++ b/solution.py
@@ -2,10 +2,19 @@
 import jax.numpy as jnp
 from jax import lax
 from jax.sharding import PartitionSpec as P
+from jax.lax import psum
 
 NX = 64
 DEGREE = 2
 NS_ITERS = 2
+
+
+def _update_field(xs):
+    row_axis = "band"
+    named_axis = "grid"
+    for it in (named_axis, row_axis):
+        xs = psum(xs, it)
+    return xs
 
 
 def with_halo(block, sides, width):
@@ -55,7 +64,7 @@
         )
         / total_cells
     )
-    gram = lax.psum(partial_value, ("band", "grid"))
+    gram = _update_field(partial_value)
     scale = jnp.max(jnp.sum(jnp.abs(gram), axis=1))
     identity_mat = jnp.eye(gram.shape[0], dtype=jnp.float32)
     upper = gram / scale

time: 103 us -> 109 us (1.058)
  blocking collectives: 56.9 us -> 63.3 us
    psum x1 -> x2, blocking collectives: 39 us -> 46.3 us  [_update_field(): xs = psum(xs, it)]
where the time goes in v1:
time: 109 us
  blocking collectives  63.3 us (58%)
  waiting for transfers between devices  15.7 us (14%)
  starting transfers between devices  9.52 us (9%)
  local copies, waits for them, and re-layouts  9.32 us (9%)
  other arithmetic  7.48 us (7%)
  matrix products  2.54 us (2%)
    psum x2, blocking collectives, _update_field(): xs = psum(xs, it)  46.3 us
    ppermute x2, waiting for transfers between devices, with_halo(): lax.ppermute(lax.slice_in_dim(block, 0, width, axis=dim), axis, backward)  10.5 us
    ppermute x2, starting transfers between devices, with_halo(): lax.ppermute(lax.slice_in_dim(block, 0, width, axis=dim), axis, backward)  9.51 us
    all_to_all x1, blocking collectives, local(): lax.all_to_all(filtered, 'band', split_axis=1, concat_axis=0, tiled=True)  8.59 us
    all_to_all x1, blocking collectives, local(): lax.all_to_all(turned, 'band', split_axis=0, concat_axis=1, tiled=True)  8.39 us
    ppermute x2, waiting for transfers between devices, with_halo(): lax.ppermute(lax.slice_in_dim(block, block.shape[dim] - width, None, axis...  5.27 us
    slice x2, local copies, waits for them, and re-layouts, with_halo(): lax.slice_in_dim(block, 0, width, axis=dim)  3.22 us
    convert_element_type x1, other arithmetic, local(): filtered = current.astype(jnp.bfloat16).reshape(count, zplanes * width)  2.58 us
  transfers between devices with their start and end apart: 4, of which 4 were waited for; matrix products, arithmetic and copies ran while one was open for 4% of the time, Pallas kernels for 0%

profile of v1, /device:TPU:0, one launch (start us, length us, event | category | flops | bytes accessed | tf_op | source)
XLA Modules:
  0.0 108.8 jit_solution(18422071424940415079)
XLA Ops:
  0.0 1.9 %fusion.24 = (f32[16,1,4096]{2,1,0:T(1,128)S(1)}, f32[16,1,4096]{2,1,0:T(1,128)S(1)}) fusion(f32[16,2,4096]{2,1,0:T(2,128)} %param.2), kind=kLoop, calls=%fused_computation.42 | loop fusion | bytes 1048576 | tf_op jit(solution)/shard_map/slice | solution.py:29
  1.9 6.1 %collective-permute-start = (f32[16,1,4096]{2,1,0:T(1,128)S(1)}, f32[16,1,4096]{2,1,0:T(1,128)S(1)}, u32[]{:S(2)}, u32[]{:S(2)}) collective-permute-start(f32[16,1,4096]{2,1,0:T(1,128)S(1)} %get-tuple-element.25), channel_id=1, source_target_pairs={{1,0},{2,1},{3,2},{4,3},{5,4},{6,5},{7,6},{0,7},{9,8},{10,9},{11,1... | collective-permute-start | bytes 786440 | tf_op jit(solution)/shard_map/ppermute | solution.py:29
  7.9 0.6 reshape.35
  9.5 0.5 copy-done.1
  10.1 0.9 fusion.4
  11.0 0.5 add.60
  11.5 2.0 %collective-permute-done = f32[16,1,4096]{2,1,0:T(1,128)S(1)} collective-permute-done((f32[16,1,4096]{2,1,0:T(1,128)S(1)}, f32[16,1,4096]{2,1,0:T(1,128)S(1)}, u32[]{:S(2)}, u32[]{:S(2)}) %collective-permute-start) | collective-permute-done | bytes 262176 | tf_op jit(solution)/shard_map/ppermute | solution.py:29
  13.5 5.0 %collective-permute-done.1 = f32[16,1,4096]{2,1,0:T(1,128)} collective-permute-done((f32[16,1,4096]{2,1,0:T(1,128)S(1)}, f32[16,1,4096]{2,1,0:T(1,128)}, u32[]{:S(2)}, u32[]{:S(2)}) %collective-permute-start.1) | collective-permute-done | bytes 262176 | tf_op jit(solution)/shard_map/ppermute | solution.py:26
  18.5 2.4 %broadcast_multiply_fusion = (f32[16,2,4096]{2,1,0:T(2,128)S(1)}, f32[16,2,4096]{2,1,0:T(2,128)S(1)}) fusion(f32[16,2,4096]{2,1,0:T(2,128)S(1)} %copy-done, f32[2,4096]{1,0:T(2,128)S(1)} %copy-done.1, f32[16,2,4096]{2,1,0:T(2,128)S(1)} %add.60, f32[16,1,4096]{2,1,0:T(1,128)} %collective-permute-done.1, f32[16,1,4096]{2,1,0:T(1,128)S(1)} %collective-permute-done), kind=kLoop, calls=%fused_computation.26 | loop fusion | flops 1572864 | bytes 2654208 | tf_op jit(solution)/shard_map/div | solution.py:52
  21.0 0.6 reshape.36
  22.5 1.3 %fusion.23 = (f32[16,1,4096]{2,1,0:T(1,128)}, f32[16,1,4096]{2,1,0:T(1,128)}) fusion(f32[16,2,4096]{2,1,0:T(2,128)S(1)} %get-tuple-element.5), kind=kLoop, calls=%fused_computation.41 | loop fusion | bytes 1048576 | tf_op jit(solution)/shard_map/slice | solution.py:29
  23.9 3.5 %collective-permute-start.2 = (f32[16,1,4096]{2,1,0:T(1,128)}, f32[16,1,4096]{2,1,0:T(1,128)S(1)}, u32[]{:S(2)}, u32[]{:S(2)}) collective-permute-start(f32[16,1,4096]{2,1,0:T(1,128)} %get-tuple-element.23), channel_id=1, source_target_pairs={{1,0},{2,1},{3,2},{4,3},{5,4},{6,5},{7,6},{0,7},{9,8},{10,9},{11,1... | collective-permute-start | bytes 786440 | tf_op jit(solution)/shard_map/ppermute | solution.py:29
  27.4 0.9 fusion.6
  28.2 0.5 add.67
  28.8 8.5 %collective-permute-done.2 = f32[16,1,4096]{2,1,0:T(1,128)S(1)} collective-permute-done((f32[16,1,4096]{2,1,0:T(1,128)}, f32[16,1,4096]{2,1,0:T(1,128)S(1)}, u32[]{:S(2)}, u32[]{:S(2)}) %collective-permute-start.2) | collective-permute-done | bytes 262176 | tf_op jit(solution)/shard_map/ppermute | solution.py:29
  37.5 2.6 %subtract_convert_fusion = bf16[16,2,4096]{2,1,0:T(2,128)(2,1)S(1)} fusion(f32[16,2,4096]{2,1,0:T(2,128)S(1)} %copy-done, f32[16,2,4096]{2,1,0:T(2,128)S(1)} %get-tuple-element.6, f32[16,2,4096]{2,1,0:T(2,128)S(1)} %add.67, f32[16,2,4096]{2,1,0:T(2,128)S(1)} %get-tuple-element.5, f32[16,1,4096]{2,1,0:T(1,128)} %collective-permute-done.3, ...), kind=kLoop, calls=%fused_computation.24 | loop fusion | flops 1835008 | bytes 2916352 | tf_op jit(solution)/shard_map/convert_element_type | solution.py:58
  40.3 8.6 %all_to_all.35 = bf16[16,4,2048]{2,0,1:T(8,128)(2,1)S(1)} all-to-all(bf16[16,4,2048]{2,0,1:T(8,128)(2,1)S(1)} %copy.7), channel_id=1, replica_groups=mesh['band'=4,'grid'=8] {'band'}, dimensions={1} | all-to-all | bytes 524288 | tf_op jit(solution)/shard_map/all_to_all | solution.py:59
  49.1 36.1 %psum.14 = f32[64,64]{1,0:T(8,128)S(1)} all-reduce(f32[64,64]{1,0:T(8,128)S(1)} %convolution_multiply_fusion.2), channel_id=1, replica_groups=mesh['band'=4,'grid'=8] {'grid'}, use_global_device_ids=true, to_apply=%region_0.1 | all-reduce | flops 4096 | bytes 32768 | tf_op jit(solution)/shard_map/psum | solution.py:16
  85.2 10.3 %psum.15 = f32[64,64]{1,0:T(8,128)S(1)} all-reduce(f32[64,64]{1,0:T(8,128)S(1)} %psum.14), channel_id=1, replica_groups=mesh['band'=4,'grid'=8] {'band'}, use_global_device_ids=true, to_apply=%region_1.2 | all-reduce | flops 4096 | bytes 32768 | tf_op jit(solution)/shard_map/psum | solution.py:16
  95.6 0.6 reduce_max.9
  96.2 0.8 fusion.1
  97.0 0.8 fusion.14
  99.3 8.4 %all_to_all.36 = bf16[4,16,2048]{2,1,0:T(8,128)(2,1)S(1)} all-to-all(bf16[4,16,2048]{2,1,0:T(8,128)(2,1)S(1)} %bitcast.21), channel_id=1, replica_groups=mesh['band'=4,'grid'=8] {'band'}, dimensions={0} | all-to-all | bytes 524288 | tf_op jit(solution)/shard_map/all_to_all | solution.py:81
  107.9 0.9 reshape.37
  (24 shorter events, 3.7 us)
Async XLA Ops:
  0.0 7.9 %copy-start = (f32[16,2,4096]{2,1,0:T(2,128)S(1)}, f32[16,2,4096]{2,1,0:T(2,128)}, u32[]{:S(2)}) copy-start(f32[16,2,4096]{2,1,0:T(2,128)} %param.2) | copy-start | bytes 1572868
  1.9 11.6 %collective-permute-start = (f32[16,1,4096]{2,1,0:T(1,128)S(1)}, f32[16,1,4096]{2,1,0:T(1,128)S(1)}, u32[]{:S(2)}, u32[]{:S(2)}) collective-permute-start(f32[16,1,4096]{2,1,0:T(1,128)S(1)} %get-tuple-element.25), channel_id=1, source_target_pairs={{1,0},{2,1},{3,2},{4,3},{5,4},{6,5},{7,6},{0,7},{9,8},{10,9},{11,1... | collective-permute-start | bytes 786440 | tf_op jit(solution)/shard_map/ppermute | solution.py:29
  7.9 10.6 %collective-permute-start.1 = (f32[16,1,4096]{2,1,0:T(1,128)S(1)}, f32[16,1,4096]{2,1,0:T(1,128)}, u32[]{:S(2)}, u32[]{:S(2)}) collective-permute-start(f32[16,1,4096]{2,1,0:T(1,128)S(1)} %get-tuple-element.26), channel_id=1, source_target_pairs={{0,1},{1,2},{2,3},{3,4},{4,5},{5,6},{6,7},{7,0},{8,9},{9,10},{10,1... | collective-permute-start | bytes 786440 | tf_op jit(solution)/shard_map/ppermute | solution.py:26
  9.3 0.8 copy-start.1
  23.9 13.4 %collective-permute-start.2 = (f32[16,1,4096]{2,1,0:T(1,128)}, f32[16,1,4096]{2,1,0:T(1,128)S(1)}, u32[]{:S(2)}, u32[]{:S(2)}) collective-permute-start(f32[16,1,4096]{2,1,0:T(1,128)} %get-tuple-element.23), channel_id=1, source_target_pairs={{1,0},{2,1},{3,2},{4,3},{5,4},{6,5},{7,6},{0,7},{9,8},{10,9},{11,1... | collective-permute-start | bytes 786440 | tf_op jit(solution)/shard_map/ppermute | solution.py:29
  27.3 10.2 %collective-permute-start.3 = (f32[16,1,4096]{2,1,0:T(1,128)}, f32[16,1,4096]{2,1,0:T(1,128)}, u32[]{:S(2)}, u32[]{:S(2)}) collective-permute-start(f32[16,1,4096]{2,1,0:T(1,128)} %get-tuple-element.24), channel_id=1, source_target_pairs={{0,1},{1,2},{2,3},{3,4},{4,5},{5,6},{6,7},{7,0},{8,9},{9,10},{10,1... | collective-permute-start | bytes 786440 | tf_op jit(solution)/shard_map/ppermute | solution.py:26
